TPU v7x, 128 devices: a whole 4x4x4 slice. The times are simulated.
128 devices in a mesh: energy: 8 (over y, core), layer: 16 (over x, z).
Axes of the slice: x: 4, y: 4, z: 4, core: 2. Of those that a mesh axis runs over, the one named last changes fastest.
Arguments:
- correlations: bfloat16 [128, 16, 4, 256, 256], P(('energy', 'layer')), may hold values from -6 to 6
- retarded: bfloat16 [128, 16, 2, 256, 256], P(('energy', 'layer')), may hold values from -0.15625 to 0.15625
- coupling: bfloat16 [16, 256, 256], P('layer'), may hold values from -0.375 to 0.375
- phonon_shifts: int32 [4], replicated, may hold values from 1 to 4, as said below
- phonon_coupling: float32 [4], replicated, may hold values from 0.3 to 1.2
- layer_orbitals: int32 [16], P('layer'), may hold values from 128 to 256, as said below
Outputs:
- left_correlations: bfloat16 [128, 16, 4, 256, 256], P('energy', 'layer')
Inputs may be any that keep to these rules, and one draw needn't show every extreme that they name: `phonon_shifts`: one of the offsets equals 4. `layer_orbitals`: some layer has all 256 orbitals live.
All inputs are finite; a program needn't handle non-finite values.
Results may differ from a plain program's by a relative error of at most 0.025.
Values may be sent and summed in bfloat16 or wider, within the bound.
No kernel may reach another device: no remote copies, remote signals or barrier semaphores. Data moves between devices by JAX's collectives and lax.ppermute only.
A program may use at most 128 MiB of HBM per device.

v0:
```python
import jax
import jax.numpy as jnp
from jax import lax
from jax.sharding import PartitionSpec as P

MODES = 4
SHIFT_MAX = 4
bose_ratio = 0.5


def with_halo(block, sides, width):
    for axis, dim in sides:
        count = lax.axis_size(axis)
        forward = [(i, i + 1) for i in range(count - 1)]
        backward = [(target, source) for source, target in forward]
        low = lax.ppermute(
            lax.slice_in_dim(block, block.shape[dim] - width, None, axis=dim), axis, forward
        )
        high = lax.ppermute(lax.slice_in_dim(block, 0, width, axis=dim), axis, backward)
        block = jnp.concatenate([low, block, high], axis=dim)
    return block


def mode_weights(shift_value):
    occupation = 1.0 / (jnp.exp(bose_ratio * shift_value.astype(jnp.float32)) - 1.0)
    lower_weight = jnp.stack([occupation, occupation, occupation + 1.0, occupation + 1.0])
    upper_weight = jnp.stack([occupation + 1.0, occupation + 1.0, occupation, occupation])
    return (lower_weight, upper_weight)


def left_product(matrix, stacked_block):
    return jnp.einsum(
        "...ab,...kbc->...kac", matrix, stacked_block, preferred_element_type=jnp.float32
    )


def right_product(stacked_block, matrix):
    return jnp.einsum(
        "...kab,...cb->...kac", stacked_block, matrix, preferred_element_type=jnp.float32
    )


def advance(previous, sigma_block, green_block, coupling_block):
    halfway = jnp.einsum(
        "...kab,cb->...kac", previous, coupling_block, preferred_element_type=jnp.float32
    ).astype(jnp.bfloat16)
    spread = jnp.einsum(
        "ab,...kbc->...kac", coupling_block, halfway, preferred_element_type=jnp.float32
    )
    source = (sigma_block.astype(jnp.float32) + spread).astype(jnp.bfloat16)
    green_real = green_block[..., 0, :, :]
    green_imag = green_block[..., 1, :, :]
    source_real = source[..., 0::2, :, :]
    source_imag = source[..., 1::2, :, :]
    inner_real = (
        left_product(green_real, source_real) - left_product(green_imag, source_imag)
    ).astype(jnp.bfloat16)
    inner_imag = (
        left_product(green_real, source_imag) + left_product(green_imag, source_real)
    ).astype(jnp.bfloat16)
    outer_real = right_product(inner_real, green_real) + right_product(inner_imag, green_imag)
    outer_imag = right_product(inner_imag, green_real) - right_product(inner_real, green_imag)
    stacked = jnp.stack([outer_real, outer_imag], axis=-3)
    return stacked.reshape(stacked.shape[:-4] + (4,) + stacked.shape[-2:]).astype(jnp.bfloat16)


def body(correlations, retarded, coupling, phonon_shifts, phonon_coupling, layer_orbitals):
    regrouped = lax.all_to_all(correlations, "layer", split_axis=1, concat_axis=0, tiled=True)
    energies_here = regrouped.shape[0]
    orbital_count = regrouped.shape[-1]
    padded = with_halo(regrouped, (("energy", 0),), SHIFT_MAX)
    accumulated = jnp.zeros(regrouped.shape, jnp.float32)
    for mode_index in range(MODES):
        shift_value = phonon_shifts[mode_index]
        lower_weight, upper_weight = mode_weights(shift_value)
        lower_block = lax.dynamic_slice_in_dim(padded, SHIFT_MAX - shift_value, energies_here, 0)
        upper_block = lax.dynamic_slice_in_dim(padded, SHIFT_MAX + shift_value, energies_here, 0)
        accumulated = accumulated + phonon_coupling[mode_index] * (
            lower_weight[:, None, None] * lower_block.astype(jnp.float32)
            + upper_weight[:, None, None] * upper_block.astype(jnp.float32)
        )
    orbital_index = jnp.arange(orbital_count, dtype=jnp.int32)
    live_count = layer_orbitals[:, None, None, None]
    live_mask = (orbital_index[:, None] < live_count) & (orbital_index[None, :] < live_count)
    sigma_blocks = jnp.where(live_mask, accumulated, 0.0).astype(jnp.bfloat16)
    returned = lax.all_to_all(sigma_blocks, "layer", split_axis=0, concat_axis=1, tiled=True)
    couplings = lax.all_gather(coupling, "layer", axis=0, tiled=True)
    layer_total = returned.shape[1]

    def layer_step(layer_index, state):
        previous, finished = state
        current = advance(
            previous,
            lax.dynamic_index_in_dim(returned, layer_index, 1, keepdims=False),
            lax.dynamic_index_in_dim(retarded, layer_index, 1, keepdims=False),
            lax.dynamic_index_in_dim(couplings, layer_index, 0, keepdims=False),
        )
        finished = lax.dynamic_update_index_in_dim(finished, current, layer_index, 1)
        return (current, finished)

    _, finished = lax.fori_loop(
        0, layer_total, layer_step, (correlations[:, 0], jnp.zeros_like(correlations))
    )
    return lax.all_to_all(finished, "layer", split_axis=1, concat_axis=0, tiled=True)


def solution(mesh):
    return jax.shard_map(
        body,
        mesh=mesh,
        in_specs=(
            P(("energy", "layer"), None, None, None, None),
            P(("energy", "layer"), None, None, None, None),
            P("layer", None, None),
            P(),
            P(),
            P("layer"),
        ),
        out_specs=P("energy", "layer", None, None, None),
        check_vma=False,
    )
```

profile of v0, /device:TPU:8, one launch (start us, length us, event | category | flops | bytes accessed | tf_op | source)
XLA Modules:
  0.0 559.1 jit_solution(11851508432102478930)
XLA Ops:
  6.5 12.2 %copy.25 = bf16[1,16,4,256,256]{3,4,2,0,1:T(8,128)(2,1)} copy(bf16[1,16,4,256,256]{4,3,2,1,0:T(8,128)(2,1)} %param.8) | data formatting | bytes 16777216 | tf_op args[0]
  18.8 104.3 %all_to_all.39 = bf16[1,16,4,256,256]{3,4,2,0,1:T(8,128)(2,1)S(1)} all-to-all(bf16[1,16,4,256,256]{3,4,2,0,1:T(8,128)(2,1)} %copy.25), channel_id=1, replica_groups=mesh['energy'=8,'layer'=16] {'layer'}, dimensions={1} | all-to-all | bytes 16777216 | tf_op jit(solution)/shard_map/all_to_all | solution.py:68
  123.1 1.6 slice_bitcast_fusion.11
  124.7 2.4 copy-done
  127.1 1.5 slice_bitcast_fusion.10
  128.6 1.9 collective-permute-start.1
  130.6 2.4 collective-permute-start
  148.3 6.1 %collective-permute-done.1 = bf16[4,1,4,256,256]{3,4,2,0,1:T(8,128)(2,1)S(1)} collective-permute-done((bf16[4,1,4,256,256]{3,4,2,0,1:T(8,128)(2,1)}, bf16[4,1,4,256,256]{3,4,2,0,1:T(8,128)(2,1)S(1)}, u32[]{:S(2)}, u32[]{:S(2)}) %collective-permute-start.1) | collective-permute-done | bytes 2097184 | tf_op jit(solution)/shard_map/ppermute | solution.py:19
  154.4 3.8 collective-permute-done
  158.2 6.4 %pad_maximum_fusion = bf16[24,1,4,256,256]{3,4,2,0,1:T(8,128)(2,1)S(1)} fusion(bf16[4,1,4,256,256]{3,4,2,0,1:T(8,128)(2,1)} %copy-done.1, bf16[16,1,4,256,256]{3,4,2,0,1:T(8,128)(2,1)} %bitcast.174, bf16[4,1,4,256,256]{3,4,2,0,1:T(8,128)(2,1)} %collective-permute-done), kind=kLoop, calls=%fused_computation.37 | loop fusion | flops 12582912 | bytes 25165824 | tf_op jit(solution)/shard_map/concatenate | solution.py:20
  164.6 20.0 %fusion.29 = bf16[16,1,4,256,256]{3,4,2,1,0:T(8,128)(2,1)} fusion(bf16[24,1,4,256,256]{3,4,2,0,1:T(8,128)(2,1)S(1)} %pad_maximum_fusion, s32[]{:T(128)S(6)} %select_n.47, f32[4]{0:T(128)S(1)} %get-tuple-element.136, s32[]{:T(128)S(6)} %select_n.46, f32[4]{0:T(128)S(1)} %get-tuple-element.135, f32[]{:T(128)} %bitcast.51, s32[]{:T(128)S(6)} %select_n.45, ...), kind=kLoop, calls=%fused_computation.38 | loop fusion | flops 121634816 | bytes 75563184 | tf_op jit(solution)/shard_map/convert_element_type | solution.py:85
  184.6 4.7 all-to-all-start.1
  190.1 1.1 slice_bitcast_fusion.12
  191.2 142.2 %all-gather.2.cloned.1.call-done = bf16[16,256,256]{2,1,0:T(8,128)(2,1)} async-done(((bf16[1,256,256]{2,1,0:T(8,128)(2,1)}), bf16[16,256,256]{2,1,0:T(8,128)(2,1)}) %all-gather.2.cloned.1.call-update) | async-done | bytes 2097168 | tf_op jit(solution)/shard_map/all_gather | solution.py:87
  333.4 6.0 %all-to-all-done.1 = bf16[16,1,4,256,256]{3,4,2,1,0:T(8,128)(2,1)} async-done(((bf16[16,1,4,256,256]{3,4,2,1,0:T(8,128)(2,1)}), bf16[16,1,4,256,256]{3,4,2,1,0:T(8,128)(2,1)}, u32[]{:S(2)}, u32[]{:S(2)}) %all-to-all-start.1) | async-done | bytes 8388640 | tf_op jit(solution)/shard_map/all_to_all | solution.py:86
  339.3 92.7 %while.15 = (s32[]{:T(128)}, bf16[1,4,256,256]{3,2,1,0:T(8,128)(2,1)S(1)}, bf16[1,16,4,256,256]{4,3,2,1,0:T(8,128)(2,1)}, bf16[1,16,4,256,256]{3,4,2,1,0:T(8,128...) while((s32[]{:T(128)}, ...), condition=%wide.region_1.2_spmd, body=%wide.region_0.1_spmd.sunk | while | flops 807665664 | bytes 13895261 | solution.py:101
  339.3 1.0 dynamic-slice_bitcast_fusion.2
  340.3 1.7 fusion.67
  344.3 0.8 bitcast_dynamic-update-slice_fusion.2
  345.1 1.0 dynamic-slice_bitcast_fusion.2
  346.1 1.7 fusion.67
  350.1 0.8 bitcast_dynamic-update-slice_fusion.2
  350.9 1.0 dynamic-slice_bitcast_fusion.2
  351.9 1.7 fusion.67
  355.9 0.8 bitcast_dynamic-update-slice_fusion.2
  356.7 1.0 dynamic-slice_bitcast_fusion.2
  357.7 1.7 fusion.67
  361.7 0.8 bitcast_dynamic-update-slice_fusion.2
  362.5 1.0 dynamic-slice_bitcast_fusion.2
  363.5 1.7 fusion.67
  368.3 1.0 dynamic-slice_bitcast_fusion.2
  369.3 1.7 fusion.67
  373.3 0.8 bitcast_dynamic-update-slice_fusion.2
  374.1 1.0 dynamic-slice_bitcast_fusion.2
  375.1 1.7 fusion.67
  379.1 0.8 bitcast_dynamic-update-slice_fusion.2
  379.9 1.0 dynamic-slice_bitcast_fusion.2
  380.9 1.7 fusion.67
  384.9 0.8 bitcast_dynamic-update-slice_fusion.2
  385.7 1.0 dynamic-slice_bitcast_fusion.2
  386.7 1.7 fusion.67
  390.7 0.8 bitcast_dynamic-update-slice_fusion.2
  391.5 1.0 dynamic-slice_bitcast_fusion.2
  392.5 1.7 fusion.67
  396.5 0.8 bitcast_dynamic-update-slice_fusion.2
  397.3 1.0 dynamic-slice_bitcast_fusion.2
  398.3 1.7 fusion.67
  402.2 0.8 bitcast_dynamic-update-slice_fusion.2
  403.1 1.0 dynamic-slice_bitcast_fusion.2
  404.0 1.7 fusion.67
  408.0 0.8 bitcast_dynamic-update-slice_fusion.2
  408.9 1.0 dynamic-slice_bitcast_fusion.2
  409.8 1.7 fusion.67
  413.8 0.8 bitcast_dynamic-update-slice_fusion.2
  414.7 1.0 dynamic-slice_bitcast_fusion.2
  415.6 1.7 fusion.67
  419.6 0.8 bitcast_dynamic-update-slice_fusion.2
  420.5 1.0 dynamic-slice_bitcast_fusion.2
  421.4 1.7 fusion.67
  425.4 0.8 bitcast_dynamic-update-slice_fusion.2
  426.3 1.0 dynamic-slice_bitcast_fusion.2
  427.2 1.7 fusion.67
  432.0 112.4 %all_to_all.40 = bf16[1,16,4,256,256]{4,3,2,0,1:T(8,128)(2,1)} all-to-all(bf16[1,16,4,256,256]{4,3,2,0,1:T(8,128)(2,1)} %bitcast.176), channel_id=1, replica_groups=mesh['energy'=8,'layer'=16] {'layer'}, dimensions={1} | all-to-all | bytes 16777216 | tf_op jit(solution)/shard_map/all_to_all | solution.py:104
  544.4 7.8 %copy.49 = bf16[16,1,4,256,256]{4,3,2,1,0:T(8,128)(2,1)} copy(bf16[16,1,4,256,256]{4,3,2,1,0:T(8,128)(2,1)} %bitcast.175) | data formatting | bytes 16777216
  (180 shorter events, 39.6 us)
Async XLA Ops:
  18.8 114.2 %copy-start.2 = (s32[4]{0:T(128)S(1)}, s32[4]{0:T(128)}, u32[]{:S(2)}) copy-start(s32[4]{0:T(128)} %param.11) | copy-start | bytes 52
  18.8 128.8 %copy-start.3 = (f32[4]{0:T(128)S(1)}, f32[4]{0:T(128)}, u32[]{:S(2)}) copy-start(f32[4]{0:T(128)} %param.12) | copy-start | bytes 52
  123.1 4.0 copy-start
  128.6 25.8 %collective-permute-start.1 = (bf16[4,1,4,256,256]{3,4,2,0,1:T(8,128)(2,1)}, bf16[4,1,4,256,256]{3,4,2,0,1:T(8,128)(2,1)S(1)}, u32[]{:S(2)}, u32[]{:S(2)}) collective-permute-start(bf16[4,1,4,256,256]{3,4,2,0,1:T(8,128)(2,1)} %slice_bitcast_fusion.10), channel_id=1, source_target_pairs={{16,0},{32,16},{48,32},{64,48},{80,64},{96,80},{112,96},{17,1},{33... | collective-permute-start | bytes 6291464 | tf_op jit(solution)/shard_map/ppermute | solution.py:19
  130.6 27.7 %collective-permute-start = (bf16[4,1,4,256,256]{3,4,2,0,1:T(8,128)(2,1)}, bf16[4,1,4,256,256]{3,4,2,0,1:T(8,128)(2,1)}, u32[]{:S(2)}, u32[]{:S(2)}) collective-permute-start(bf16[4,1,4,256,256]{3,4,2,0,1:T(8,128)(2,1)} %slice_bitcast_fusion.11), channel_id=1, source_target_pairs={{0,16},{16,32},{32,48},{48,64},{64,80},{80,96},{96,112},{1,17},{17... | collective-permute-start | bytes 6291464 | tf_op jit(solution)/shard_map/ppermute | solution.py:16
  154.4 3.8 copy-start.1
  184.6 154.7 %all-to-all-start.1 = ((bf16[16,1,4,256,256]{3,4,2,1,0:T(8,128)(2,1)}), bf16[16,1,4,256,256]{3,4,2,1,0:T(8,128)(2,1)}, u32[]{:S(2)}, u32[]{:S(2)}) async-start(bf16[16,1,4,256,256]{3,4,2,1,0:T(8,128)(2,1)} %fusion.29), calls=%async_computation.1 | async-start | bytes 16777216 | tf_op jit(solution)/shard_map/all_to_all | solution.py:86
  189.4 144.0 %all-gather.2.cloned.1.call-start = ((), (), s32[]{:S(2)}) async-start(), calls=%async_computation.3 | async-start | bytes 2228224 | tf_op jit(solution)/shard_map/all_gather | solution.py:87
Sparse Core Ops, SparseCore 0:
  192.3 140.9 all-gather.1
where the time goes:
time: 561 us; the launch traced here: 559 us
  blocking collectives  217 us (39%)
  waiting for transfers between devices  159 us (28%)
  matrix products  61.4 us (11%)
  local copies, waits for them, and re-layouts  57.3 us (10%)
  other arithmetic  27.6 us (5%)
  between operations  27 us (5%)
  starting transfers between devices  9.1 us (2%)
    all_gather x1, waiting for transfers between devices, body(): couplings = lax.all_gather(coupling, 'layer', axis=0, tiled=True)  142 us
    all_to_all x1, blocking collectives, body(): lax.all_to_all(finished, 'layer', split_axis=1, concat_axis=0, tiled=True)  112 us
    all_to_all x1, blocking collectives, body(): lax.all_to_all(correlations, 'layer', split_axis=1, concat_axis=0, tiled=...  104 us
    dot_general x16, matrix products, advance(): jnp.einsum('ab,...kbc->...kac', coupling_block, halfway, preferred_elemen...  27.3 us
    unnamed x10, local copies, waits for them, and re-layouts  22.5 us
    convert_element_type x1, other arithmetic, body(): sigma_blocks = jnp.where(live_mask, accumulated, 0.0).astype(jnp.bfloat16)  20 us
    dot_general x64, matrix products, right_product(): jnp.einsum('...kab,...cb->...kac', stacked_block, matrix, preferred_eleme...  17.5 us
    dot_general x64, matrix products, left_product(): jnp.einsum('...ab,...kbc->...kac', matrix, stacked_block, preferred_eleme...  16.5 us
  transfers between devices with their start and end apart: 4, of which 4 were waited for; matrix products, arithmetic and copies ran while one was open for 1% of the time, Pallas kernels for 0%

commit v1 on v0

--- a/solution.py
+++ b/solution.py
@@ -84,7 +84,14 @@
     live_mask = (orbital_index[:, None] < live_count) & (orbital_index[None, :] < live_count)
     sigma_blocks = jnp.where(live_mask, accumulated, 0.0).astype(jnp.bfloat16)
     returned = lax.all_to_all(sigma_blocks, "layer", split_axis=0, concat_axis=1, tiled=True)
-    couplings = lax.all_gather(coupling, "layer", axis=0, tiled=True)
+    ring = [coupling]
+    for hop in range(15):
+        ring.append(lax.ppermute(ring[-1], "layer", [(dev, (dev + 1) % 16) for dev in range(16)]))
+    couplings = jnp.roll(
+        jnp.concatenate(ring[::-1], axis=0),
+        (lax.axis_index("layer") + 1) * ring[0].shape[0],
+        axis=0,
+    )
     layer_total = returned.shape[1]
 
     def layer_step(layer_index, state):

time: 561 us -> 600 us (1.070)
  waiting for transfers between devices: 159 us -> 223 us
  blocking collectives: 217 us -> 197 us
  between operations: 27 us -> 13.4 us
  starting transfers between devices: 9.1 us -> 19.9 us
    ppermute x0 -> x15, waiting for transfers between devices: none -> 212 us  [body(): lax.ppermute(ring[-1], 'layer', [(dev, (dev + 1) % 16) for dev in range(1...]
    all_gather x1 -> x0, waiting for transfers between devices: 142 us -> none  [body(): couplings = lax.all_gather(coupling, 'layer', axis=0, tiled=True)]
    all_to_all x1, blocking collectives: 112 us -> 92.3 us  [body(): lax.all_to_all(finished, 'layer', split_axis=1, concat_axis=0, tiled=True)]
    ppermute x0 -> x15, starting transfers between devices: none -> 10.7 us  [body(): lax.ppermute(ring[-1], 'layer', [(dev, (dev + 1) % 16) for dev in range(1...]
    unnamed x10 -> x43, local copies, waits for them, and re-layouts: 22.5 us -> 21.4 us
  transfers between devices with their start and end apart: 4 -> 18, of which waited for: 4 -> 17; matrix products, arithmetic and copies ran while one was open for 1% -> 1% of each run, Pallas kernels for 0% -> 0%
where the time goes in v1:
time: 600 us; the launch traced here: 598 us
  waiting for transfers between devices  223 us (37%)
  blocking collectives  197 us (33%)
  matrix products  59.2 us (10%)
  local copies, waits for them, and re-layouts  56.9 us (9%)
  other arithmetic  27.8 us (5%)
  starting transfers between devices  19.9 us (3%)
  between operations  13.4 us (2%)
    ppermute x15, waiting for transfers between devices, body(): lax.ppermute(ring[-1], 'layer', [(dev, (dev + 1) % 16) for dev in range(1...  212 us
    all_to_all x1, blocking collectives, body(): lax.all_to_all(correlations, 'layer', split_axis=1, concat_axis=0, tiled=...  104 us
    all_to_all x1, blocking collectives, body(): lax.all_to_all(finished, 'layer', split_axis=1, concat_axis=0, tiled=True)  92.3 us
    dot_general x16, matrix products, advance(): jnp.einsum('ab,...kbc->...kac', coupling_block, halfway, preferred_elemen...  25 us
    unnamed x43, local copies, waits for them, and re-layouts  21.4 us
    convert_element_type x1, other arithmetic, body(): sigma_blocks = jnp.where(live_mask, accumulated, 0.0).astype(jnp.bfloat16)  20.2 us
    dot_general x64, matrix products, right_product(): jnp.einsum('...kab,...cb->...kac', stacked_block, matrix, preferred_eleme...  17.5 us
    dot_general x64, matrix products, left_product(): jnp.einsum('...ab,...kbc->...kac', matrix, stacked_block, preferred_eleme...  16.6 us
  transfers between devices with their start and end apart: 18, of which 17 were waited for; matrix products, arithmetic and copies ran while one was open for 1% of the time, Pallas kernels for 0%

profile of v1, /device:TPU:8, one launch (start us, length us, event | category | flops | bytes accessed | tf_op | source)
XLA Modules:
  0.0 597.7 jit_solution(4149869393702816642)
XLA Ops:
  0.0 12.2 %copy.25 = bf16[1,16,4,256,256]{3,4,2,0,1:T(8,128)(2,1)} copy(bf16[1,16,4,256,256]{4,3,2,1,0:T(8,128)(2,1)} %param.8) | data formatting | bytes 16777216 | tf_op args[0]
  12.2 104.2 %all_to_all.39 = bf16[1,16,4,256,256]{3,4,2,0,1:T(8,128)(2,1)S(1)} all-to-all(bf16[1,16,4,256,256]{3,4,2,0,1:T(8,128)(2,1)} %copy.25), channel_id=1, replica_groups=mesh['energy'=8,'layer'=16] {'layer'}, dimensions={1} | all-to-all | bytes 16777216 | tf_op jit(solution)/shard_map/all_to_all | solution.py:68
  116.4 1.6 slice_bitcast_fusion.11
  118.0 2.0 slice_bitcast_fusion.10
  120.1 1.0 copy-done
  121.1 1.9 collective-permute-start.1
  123.0 2.4 collective-permute-start
  140.2 6.6 %collective-permute-done.1 = bf16[4,1,4,256,256]{3,4,2,0,1:T(8,128)(2,1)S(1)} collective-permute-done((bf16[4,1,4,256,256]{3,4,2,0,1:T(8,128)(2,1)}, bf16[4,1,4,256,256]{3,4,2,0,1:T(8,128)(2,1)S(1)}, u32[]{:S(2)}, u32[]{:S(2)}) %collective-permute-start.1) | collective-permute-done | bytes 2097184 | tf_op jit(solution)/shard_map/ppermute | solution.py:19
  146.9 3.8 collective-permute-done
  150.7 6.4 %pad_maximum_fusion = bf16[24,1,4,256,256]{3,4,2,0,1:T(8,128)(2,1)S(1)} fusion(bf16[4,1,4,256,256]{3,4,2,0,1:T(8,128)(2,1)} %copy-done.1, bf16[16,1,4,256,256]{3,4,2,0,1:T(8,128)(2,1)} %bitcast.174, bf16[4,1,4,256,256]{3,4,2,0,1:T(8,128)(2,1)} %collective-permute-done), kind=kLoop, calls=%fused_computation.37 | loop fusion | flops 12582912 | bytes 25165824 | tf_op jit(solution)/shard_map/concatenate | solution.py:20
  157.1 20.2 %fusion.29 = bf16[16,1,4,256,256]{3,4,2,1,0:T(8,128)(2,1)} fusion(bf16[24,1,4,256,256]{3,4,2,0,1:T(8,128)(2,1)S(1)} %pad_maximum_fusion, s32[]{:T(128)S(6)} %select_n.60, f32[4]{0:T(128)S(1)} %get-tuple-element.136, s32[]{:T(128)S(6)} %select_n.59, f32[4]{0:T(128)S(1)} %get-tuple-element.135, f32[]{:T(128)} %bitcast.51, s32[]{:T(128)S(6)} %select_n.58, ...), kind=kLoop, calls=%fused_computation.38 | loop fusion | flops 121634816 | bytes 75563184 | tf_op jit(solution)/shard_map/convert_element_type | solution.py:85
  177.2 4.9 all-to-all-start.1
  182.2 1.8 collective-permute-start.2
  184.0 103.0 %collective-permute-done.2 = bf16[1,256,256]{2,1,0:T(8,128)(2,1)S(1)} collective-permute-done((bf16[1,256,256]{2,1,0:T(8,128)(2,1)S(1)}, bf16[1,256,256]{2,1,0:T(8,128)(2,1)S(1)}, u32[]{:S(2)}, u32[]{:S(2)}) %collective-permute-start.2) | collective-permute-done | bytes 131104 | tf_op jit(solution)/shard_map/ppermute | solution.py:89
  287.0 8.3 %collective-permute-done.3 = bf16[1,256,256]{2,1,0:T(8,128)(2,1)S(1)} collective-permute-done((bf16[1,256,256]{2,1,0:T(8,128)(2,1)S(1)}, bf16[1,256,256]{2,1,0:T(8,128)(2,1)S(1)}, u32[]{:S(2)}, u32[]{:S(2)}) %collective-permute-start.3) | collective-permute-done | bytes 131104 | tf_op jit(solution)/shard_map/ppermute | solution.py:89
  295.2 9.1 %collective-permute-done.4 = bf16[1,256,256]{2,1,0:T(8,128)(2,1)S(1)} collective-permute-done((bf16[1,256,256]{2,1,0:T(8,128)(2,1)S(1)}, bf16[1,256,256]{2,1,0:T(8,128)(2,1)S(1)}, u32[]{:S(2)}, u32[]{:S(2)}) %collective-permute-start.4) | collective-permute-done | bytes 131104 | tf_op jit(solution)/shard_map/ppermute | solution.py:89
  304.4 2.5 collective-permute-start.5
  306.9 6.3 %collective-permute-done.5 = bf16[1,256,256]{2,1,0:T(8,128)(2,1)S(1)} collective-permute-done((bf16[1,256,256]{2,1,0:T(8,128)(2,1)S(1)}, bf16[1,256,256]{2,1,0:T(8,128)(2,1)S(1)}, u32[]{:S(2)}, u32[]{:S(2)}) %collective-permute-start.5) | collective-permute-done | bytes 131104 | tf_op jit(solution)/shard_map/ppermute | solution.py:89
  313.1 4.6 collective-permute-start.6
  317.7 3.7 collective-permute-done.6
  321.4 1.8 collective-permute-start.7
  323.2 6.5 %collective-permute-done.7 = bf16[1,256,256]{2,1,0:T(8,128)(2,1)S(1)} collective-permute-done((bf16[1,256,256]{2,1,0:T(8,128)(2,1)S(1)}, bf16[1,256,256]{2,1,0:T(8,128)(2,1)S(1)}, u32[]{:S(2)}, u32[]{:S(2)}) %collective-permute-start.7) | collective-permute-done | bytes 131104 | tf_op jit(solution)/shard_map/ppermute | solution.py:89
  329.7 8.3 %collective-permute-done.8 = bf16[1,256,256]{2,1,0:T(8,128)(2,1)S(1)} collective-permute-done((bf16[1,256,256]{2,1,0:T(8,128)(2,1)S(1)}, bf16[1,256,256]{2,1,0:T(8,128)(2,1)S(1)}, u32[]{:S(2)}, u32[]{:S(2)}) %collective-permute-start.8) | collective-permute-done | bytes 131104 | tf_op jit(solution)/shard_map/ppermute | solution.py:89
  338.0 8.3 %collective-permute-done.9 = bf16[1,256,256]{2,1,0:T(8,128)(2,1)S(1)} collective-permute-done((bf16[1,256,256]{2,1,0:T(8,128)(2,1)S(1)}, bf16[1,256,256]{2,1,0:T(8,128)(2,1)S(1)}, u32[]{:S(2)}, u32[]{:S(2)}) %collective-permute-start.9) | collective-permute-done | bytes 131104 | tf_op jit(solution)/shard_map/ppermute | solution.py:89
  346.3 8.3 %collective-permute-done.10 = bf16[1,256,256]{2,1,0:T(8,128)(2,1)S(1)} collective-permute-done((bf16[1,256,256]{2,1,0:T(8,128)(2,1)S(1)}, bf16[1,256,256]{2,1,0:T(8,128)(2,1)S(1)}, u32[]{:S(2)}, u32[]{:S(2)}) %collective-permute-start.10) | collective-permute-done | bytes 131104 | tf_op jit(solution)/shard_map/ppermute | solution.py:89
  354.6 8.3 %collective-permute-done.11 = bf16[1,256,256]{2,1,0:T(8,128)(2,1)S(1)} collective-permute-done((bf16[1,256,256]{2,1,0:T(8,128)(2,1)S(1)}, bf16[1,256,256]{2,1,0:T(8,128)(2,1)S(1)}, u32[]{:S(2)}, u32[]{:S(2)}) %collective-permute-start.11) | collective-permute-done | bytes 131104 | tf_op jit(solution)/shard_map/ppermute | solution.py:89
  362.9 8.4 %collective-permute-done.12 = bf16[1,256,256]{2,1,0:T(8,128)(2,1)S(1)} collective-permute-done((bf16[1,256,256]{2,1,0:T(8,128)(2,1)S(1)}, bf16[1,256,256]{2,1,0:T(8,128)(2,1)S(1)}, u32[]{:S(2)}, u32[]{:S(2)}) %collective-permute-start.12) | collective-permute-done | bytes 131104 | tf_op jit(solution)/shard_map/ppermute | solution.py:89
  371.3 9.6 %collective-permute-done.13 = bf16[1,256,256]{2,1,0:T(8,128)(2,1)S(1)} collective-permute-done((bf16[1,256,256]{2,1,0:T(8,128)(2,1)S(1)}, bf16[1,256,256]{2,1,0:T(8,128)(2,1)S(1)}, u32[]{:S(2)}, u32[]{:S(2)}) %collective-permute-start.13) | collective-permute-done | bytes 131104 | tf_op jit(solution)/shard_map/ppermute | solution.py:89
  380.8 8.8 %collective-permute-done.14 = bf16[1,256,256]{2,1,0:T(8,128)(2,1)S(1)} collective-permute-done((bf16[1,256,256]{2,1,0:T(8,128)(2,1)S(1)}, bf16[1,256,256]{2,1,0:T(8,128)(2,1)S(1)}, u32[]{:S(2)}, u32[]{:S(2)}) %collective-permute-start.14) | collective-permute-done | bytes 131104 | tf_op jit(solution)/shard_map/ppermute | solution.py:89
  389.7 8.3 %collective-permute-done.15 = bf16[1,256,256]{2,1,0:T(8,128)(2,1)S(1)} collective-permute-done((bf16[1,256,256]{2,1,0:T(8,128)(2,1)S(1)}, bf16[1,256,256]{2,1,0:T(8,128)(2,1)S(1)}, u32[]{:S(2)}, u32[]{:S(2)}) %collective-permute-start.15) | collective-permute-done | bytes 131104 | tf_op jit(solution)/shard_map/ppermute | solution.py:89
  397.9 1.1 slice_bitcast_fusion.12
  399.0 7.2 %collective-permute-done.16 = bf16[1,256,256]{2,1,0:T(8,128)(2,1)S(1)} collective-permute-done((bf16[1,256,256]{2,1,0:T(8,128)(2,1)S(1)}, bf16[1,256,256]{2,1,0:T(8,128)(2,1)S(1)}, u32[]{:S(2)}, u32[]{:S(2)}) %collective-permute-start.16) | collective-permute-done | bytes 131104 | tf_op jit(solution)/shard_map/ppermute | solution.py:89
  407.0 90.6 %while.15 = (s32[]{:T(128)}, bf16[1,4,256,256]{3,2,1,0:T(8,128)(2,1)S(1)}, bf16[1,16,4,256,256]{4,3,2,1,0:T(8,128)(2,1)}, bf16[1,16,4,256,256]{3,4,2,1,0:T(8,128...) while((s32[]{:T(128)}, ...), condition=%wide.region_1.2_spmd, body=%wide.region_0.1_spmd.sunk | while | flops 807665664 | bytes 13895261 | solution.py:108
  407.0 1.0 dynamic-slice_bitcast_fusion.2
  408.0 1.6 fusion.67
  412.7 1.0 dynamic-slice_bitcast_fusion.2
  413.6 1.6 fusion.67
  418.3 1.0 dynamic-slice_bitcast_fusion.2
  419.3 1.6 fusion.67
  424.0 1.0 dynamic-slice_bitcast_fusion.2
  425.0 1.6 fusion.67
  429.7 1.0 dynamic-slice_bitcast_fusion.2
  430.6 1.6 fusion.67
  435.3 1.0 dynamic-slice_bitcast_fusion.2
  436.3 1.6 fusion.67
  441.0 1.0 dynamic-slice_bitcast_fusion.2
  441.9 1.6 fusion.67
  446.6 1.0 dynamic-slice_bitcast_fusion.2
  447.6 1.6 fusion.67
  452.3 1.0 dynamic-slice_bitcast_fusion.2
  453.3 1.6 fusion.67
  457.9 1.0 dynamic-slice_bitcast_fusion.2
  458.9 1.6 fusion.67
  463.6 1.0 dynamic-slice_bitcast_fusion.2
  464.6 1.6 fusion.67
  469.3 1.0 dynamic-slice_bitcast_fusion.2
  470.2 1.6 fusion.67
  474.9 1.0 dynamic-slice_bitcast_fusion.2
  475.9 1.6 fusion.67
  481.6 1.6 fusion.67
  487.2 1.6 fusion.67
  492.9 1.6 fusion.67
  497.6 92.3 %all_to_all.40 = bf16[1,16,4,256,256]{4,3,2,0,1:T(8,128)(2,1)} all-to-all(bf16[1,16,4,256,256]{4,3,2,0,1:T(8,128)(2,1)} %bitcast.176), channel_id=1, replica_groups=mesh['energy'=8,'layer'=16] {'layer'}, dimensions={1} | all-to-all | bytes 16777216 | tf_op jit(solution)/shard_map/all_to_all | solution.py:111
  589.9 7.8 %copy.80 = bf16[16,1,4,256,256]{4,3,2,1,0:T(8,128)(2,1)} copy(bf16[16,1,4,256,256]{4,3,2,1,0:T(8,128)(2,1)} %bitcast.175) | data formatting | bytes 16777216
  (242 shorter events, 54.1 us)
Async XLA Ops:
  116.4 4.7 copy-start
  116.4 9.0 %copy-start.3 = (s32[4]{0:T(128)S(1)}, s32[4]{0:T(128)}, u32[]{:S(2)}) copy-start(s32[4]{0:T(128)} %param.11) | copy-start | bytes 52
  116.4 23.0 %copy-start.4 = (f32[4]{0:T(128)S(1)}, f32[4]{0:T(128)}, u32[]{:S(2)}) copy-start(f32[4]{0:T(128)} %param.12) | copy-start | bytes 52
  121.1 25.8 %collective-permute-start.1 = (bf16[4,1,4,256,256]{3,4,2,0,1:T(8,128)(2,1)}, bf16[4,1,4,256,256]{3,4,2,0,1:T(8,128)(2,1)S(1)}, u32[]{:S(2)}, u32[]{:S(2)}) collective-permute-start(bf16[4,1,4,256,256]{3,4,2,0,1:T(8,128)(2,1)} %slice_bitcast_fusion.10), channel_id=1, source_target_pairs={{16,0},{32,16},{48,32},{64,48},{80,64},{96,80},{112,96},{17,1},{33... | collective-permute-start | bytes 6291464 | tf_op jit(solution)/shard_map/ppermute | solution.py:19
  123.0 27.7 %collective-permute-start = (bf16[4,1,4,256,256]{3,4,2,0,1:T(8,128)(2,1)}, bf16[4,1,4,256,256]{3,4,2,0,1:T(8,128)(2,1)}, u32[]{:S(2)}, u32[]{:S(2)}) collective-permute-start(bf16[4,1,4,256,256]{3,4,2,0,1:T(8,128)(2,1)} %slice_bitcast_fusion.11), channel_id=1, source_target_pairs={{0,16},{16,32},{32,48},{48,64},{64,80},{80,96},{96,112},{1,17},{17... | collective-permute-start | bytes 6291464 | tf_op jit(solution)/shard_map/ppermute | solution.py:16
  146.9 3.8 copy-start.1
  177.2 4.9 copy-start.2
  177.2 229.8 %all-to-all-start.1 = ((bf16[16,1,4,256,256]{3,4,2,1,0:T(8,128)(2,1)}), bf16[16,1,4,256,256]{3,4,2,1,0:T(8,128)(2,1)}, u32[]{:S(2)}, u32[]{:S(2)}) async-start(bf16[16,1,4,256,256]{3,4,2,1,0:T(8,128)(2,1)} %fusion.29), calls=%async_computation.1 | async-start | bytes 16777216 | tf_op jit(solution)/shard_map/all_to_all | solution.py:86
  182.2 104.8 %collective-permute-start.2 = (bf16[1,256,256]{2,1,0:T(8,128)(2,1)S(1)}, bf16[1,256,256]{2,1,0:T(8,128)(2,1)S(1)}, u32[]{:S(2)}, u32[]{:S(2)}) collective-permute-start(bf16[1,256,256]{2,1,0:T(8,128)(2,1)S(1)} %copy-done.2), channel_id=1, source_target_pairs={{0,1},{1,2},{2,3},{3,4},{4,5},{5,6},{6,7},{7,8},{8,9},{9,10},{10,1... | collective-permute-start | bytes 393224 | tf_op jit(solution)/shard_map/ppermute | solution.py:89
  287.0 8.3 %collective-permute-start.3 = (bf16[1,256,256]{2,1,0:T(8,128)(2,1)S(1)}, bf16[1,256,256]{2,1,0:T(8,128)(2,1)S(1)}, u32[]{:S(2)}, u32[]{:S(2)}) collective-permute-start(bf16[1,256,256]{2,1,0:T(8,128)(2,1)S(1)} %collective-permute-done.2), channel_id=1, source_target_pairs={{0,1},{1,2},{2,3},{3,4},{4,5},{5,6},{6,7},{7,8},{8,9},{9,10},{10,1... | collective-permute-start | bytes 393224 | tf_op jit(solution)/shard_map/ppermute | solution.py:89
  295.2 9.1 %collective-permute-start.4 = (bf16[1,256,256]{2,1,0:T(8,128)(2,1)S(1)}, bf16[1,256,256]{2,1,0:T(8,128)(2,1)S(1)}, u32[]{:S(2)}, u32[]{:S(2)}) collective-permute-start(bf16[1,256,256]{2,1,0:T(8,128)(2,1)S(1)} %collective-permute-done.3), channel_id=1, source_target_pairs={{0,1},{1,2},{2,3},{3,4},{4,5},{5,6},{6,7},{7,8},{8,9},{9,10},{10,1... | collective-permute-start | bytes 393224 | tf_op jit(solution)/shard_map/ppermute | solution.py:89
  304.4 8.7 %collective-permute-start.5 = (bf16[1,256,256]{2,1,0:T(8,128)(2,1)S(1)}, bf16[1,256,256]{2,1,0:T(8,128)(2,1)S(1)}, u32[]{:S(2)}, u32[]{:S(2)}) collective-permute-start(bf16[1,256,256]{2,1,0:T(8,128)(2,1)S(1)} %collective-permute-done.4), channel_id=1, source_target_pairs={{0,1},{1,2},{2,3},{3,4},{4,5},{5,6},{6,7},{7,8},{8,9},{9,10},{10,1... | collective-permute-start | bytes 393224 | tf_op jit(solution)/shard_map/ppermute | solution.py:89
  313.1 8.3 %collective-permute-start.6 = (bf16[1,256,256]{2,1,0:T(8,128)(2,1)S(1)}, bf16[1,256,256]{2,1,0:T(8,128)(2,1)S(1)}, u32[]{:S(2)}, u32[]{:S(2)}) collective-permute-start(bf16[1,256,256]{2,1,0:T(8,128)(2,1)S(1)} %collective-permute-done.5), channel_id=1, source_target_pairs={{0,1},{1,2},{2,3},{3,4},{4,5},{5,6},{6,7},{7,8},{8,9},{9,10},{10,1... | collective-permute-start | bytes 393224 | tf_op jit(solution)/shard_map/ppermute | solution.py:89
  321.4 8.3 %collective-permute-start.7 = (bf16[1,256,256]{2,1,0:T(8,128)(2,1)S(1)}, bf16[1,256,256]{2,1,0:T(8,128)(2,1)S(1)}, u32[]{:S(2)}, u32[]{:S(2)}) collective-permute-start(bf16[1,256,256]{2,1,0:T(8,128)(2,1)S(1)} %collective-permute-done.6), channel_id=1, source_target_pairs={{0,1},{1,2},{2,3},{3,4},{4,5},{5,6},{6,7},{7,8},{8,9},{9,10},{10,1... | collective-permute-start | bytes 393224 | tf_op jit(solution)/shard_map/ppermute | solution.py:89
  329.7 8.3 %collective-permute-start.8 = (bf16[1,256,256]{2,1,0:T(8,128)(2,1)S(1)}, bf16[1,256,256]{2,1,0:T(8,128)(2,1)S(1)}, u32[]{:S(2)}, u32[]{:S(2)}) collective-permute-start(bf16[1,256,256]{2,1,0:T(8,128)(2,1)S(1)} %collective-permute-done.7), channel_id=1, source_target_pairs={{0,1},{1,2},{2,3},{3,4},{4,5},{5,6},{6,7},{7,8},{8,9},{9,10},{10,1... | collective-permute-start | bytes 393224 | tf_op jit(solution)/shard_map/ppermute | solution.py:89
  338.0 8.3 %collective-permute-start.9 = (bf16[1,256,256]{2,1,0:T(8,128)(2,1)S(1)}, bf16[1,256,256]{2,1,0:T(8,128)(2,1)S(1)}, u32[]{:S(2)}, u32[]{:S(2)}) collective-permute-start(bf16[1,256,256]{2,1,0:T(8,128)(2,1)S(1)} %collective-permute-done.8), channel_id=1, source_target_pairs={{0,1},{1,2},{2,3},{3,4},{4,5},{5,6},{6,7},{7,8},{8,9},{9,10},{10,1... | collective-permute-start | bytes 393224 | tf_op jit(solution)/shard_map/ppermute | solution.py:89
  346.3 8.3 %collective-permute-start.10 = (bf16[1,256,256]{2,1,0:T(8,128)(2,1)S(1)}, bf16[1,256,256]{2,1,0:T(8,128)(2,1)S(1)}, u32[]{:S(2)}, u32[]{:S(2)}) collective-permute-start(bf16[1,256,256]{2,1,0:T(8,128)(2,1)S(1)} %collective-permute-done.9), channel_id=1, source_target_pairs={{0,1},{1,2},{2,3},{3,4},{4,5},{5,6},{6,7},{7,8},{8,9},{9,10},{10,1... | collective-permute-start | bytes 393224 | tf_op jit(solution)/shard_map/ppermute | solution.py:89
  354.6 8.3 %collective-permute-start.11 = (bf16[1,256,256]{2,1,0:T(8,128)(2,1)S(1)}, bf16[1,256,256]{2,1,0:T(8,128)(2,1)S(1)}, u32[]{:S(2)}, u32[]{:S(2)}) collective-permute-start(bf16[1,256,256]{2,1,0:T(8,128)(2,1)S(1)} %collective-permute-done.10), channel_id=1, source_target_pairs={{0,1},{1,2},{2,3},{3,4},{4,5},{5,6},{6,7},{7,8},{8,9},{9,10},{10,1... | collective-permute-start | bytes 393224 | tf_op jit(solution)/shard_map/ppermute | solution.py:89
  362.8 8.4 %collective-permute-start.12 = (bf16[1,256,256]{2,1,0:T(8,128)(2,1)S(1)}, bf16[1,256,256]{2,1,0:T(8,128)(2,1)S(1)}, u32[]{:S(2)}, u32[]{:S(2)}) collective-permute-start(bf16[1,256,256]{2,1,0:T(8,128)(2,1)S(1)} %collective-permute-done.11), channel_id=1, source_target_pairs={{0,1},{1,2},{2,3},{3,4},{4,5},{5,6},{6,7},{7,8},{8,9},{9,10},{10,1... | collective-permute-start | bytes 393224 | tf_op jit(solution)/shard_map/ppermute | solution.py:89
  371.3 9.6 %collective-permute-start.13 = (bf16[1,256,256]{2,1,0:T(8,128)(2,1)S(1)}, bf16[1,256,256]{2,1,0:T(8,128)(2,1)S(1)}, u32[]{:S(2)}, u32[]{:S(2)}) collective-permute-start(bf16[1,256,256]{2,1,0:T(8,128)(2,1)S(1)} %collective-permute-done.12), channel_id=1, source_target_pairs={{0,1},{1,2},{2,3},{3,4},{4,5},{5,6},{6,7},{7,8},{8,9},{9,10},{10,1... | collective-permute-start | bytes 393224 | tf_op jit(solution)/shard_map/ppermute | solution.py:89
  380.8 8.8 %collective-permute-start.14 = (bf16[1,256,256]{2,1,0:T(8,128)(2,1)S(1)}, bf16[1,256,256]{2,1,0:T(8,128)(2,1)S(1)}, u32[]{:S(2)}, u32[]{:S(2)}) collective-permute-start(bf16[1,256,256]{2,1,0:T(8,128)(2,1)S(1)} %collective-permute-done.13), channel_id=1, source_target_pairs={{0,1},{1,2},{2,3},{3,4},{4,5},{5,6},{6,7},{7,8},{8,9},{9,10},{10,1... | collective-permute-start | bytes 393224 | tf_op jit(solution)/shard_map/ppermute | solution.py:89
  389.6 8.3 %collective-permute-start.15 = (bf16[1,256,256]{2,1,0:T(8,128)(2,1)S(1)}, bf16[1,256,256]{2,1,0:T(8,128)(2,1)S(1)}, u32[]{:S(2)}, u32[]{:S(2)}) collective-permute-start(bf16[1,256,256]{2,1,0:T(8,128)(2,1)S(1)} %collective-permute-done.14), channel_id=1, source_target_pairs={{0,1},{1,2},{2,3},{3,4},{4,5},{5,6},{6,7},{7,8},{8,9},{9,10},{10,1... | collective-permute-start | bytes 393224 | tf_op jit(solution)/shard_map/ppermute | solution.py:89
  397.9 8.3 %collective-permute-start.16 = (bf16[1,256,256]{2,1,0:T(8,128)(2,1)S(1)}, bf16[1,256,256]{2,1,0:T(8,128)(2,1)S(1)}, u32[]{:S(2)}, u32[]{:S(2)}) collective-permute-start(bf16[1,256,256]{2,1,0:T(8,128)(2,1)S(1)} %collective-permute-done.15), channel_id=1, source_target_pairs={{0,1},{1,2},{2,3},{3,4},{4,5},{5,6},{6,7},{7,8},{8,9},{9,10},{10,1... | collective-permute-start | bytes 393224 | tf_op jit(solution)/shard_map/ppermute | solution.py:89
